TPU v7x, 512 devices: a whole 4x4x16 slice. The times are simulated.
512 devices in a mesh: dp: 32 (over z, y_lo), tensor: 16 (over y_hi, x, core).
Axes of the slice: x: 4, y: 4 (y_hi: 2, y_lo: 2; y = y_hi * 2 + y_lo), z: 16, core: 2. Of those that a mesh axis runs over, the one named last changes fastest.
Arguments:
- activations: bfloat16 [32768, 8192], P('dp', 'tensor'), may hold values from -6 to 6
- out_grads: bfloat16 [32768, 8192], P('dp', 'tensor'), may hold values from -6 to 6
- proj_in: bfloat16 [8192, 64], P('tensor'), may hold values from -0.0625 to 0.0625
- proj_out: bfloat16 [8192, 64], P('tensor'), may hold values from -0.0625 to 0.0625
- segment_ids: int32 [32, 1024], P('dp'), may hold values from 0 to 23, never falling along the last dimension, each value on 1 to 80 neighbouring positions
- train_logs: bfloat16 [131072, 4096], P('dp', 'tensor'), may hold values from -6 to 6
- doc_ids: int32 [131072], P(('dp', 'tensor')), may hold values from 0 to 255
Outputs:
- scores: float32 [768, 131072], P(None, ('dp', 'tensor'))
- doc_influence: float32 [768, 256], replicated
Inputs may be any that keep to these rules, and one draw needn't show every extreme that they name: `segment_ids`: in each row the example numbers never fall; each of the 24 examples has 1 to 80 tokens, and one has exactly 80.
All inputs are finite; a program needn't handle non-finite values.
Results may differ from a plain program's by a relative error of at most 0.0052.
Values may be sent and summed in bfloat16 or wider, within the bound.
No kernel may reach another device: no remote copies, remote signals or barrier semaphores. Data moves between devices by JAX's collectives and lax.ppermute only.
A program may use at most 64 MiB of HBM per device.

v0:
```python
import math
import jax
import jax.numpy as jnp
from jax import lax
from jax.sharding import PartitionSpec as P

EX_DEV = 24
DOCS = 256


def per_device(activations, out_grads, proj_in, proj_out, segment_ids, train_logs, doc_ids):
    width_parts = lax.axis_size("tensor")
    position = lax.axis_index("tensor")
    tok_rows = activations.shape[0]
    rank = proj_in.shape[1]
    partial_value = jnp.concatenate(
        [
            jnp.dot(activations, proj_in, preferred_element_type=jnp.float32),
            jnp.dot(out_grads, proj_out, preferred_element_type=jnp.float32),
        ],
        axis=1,
    )
    seg_row = segment_ids[0]
    labels = jnp.arange(EX_DEV, dtype=jnp.int32)
    counts = jnp.sum((seg_row[:, None] == labels[None, :]).astype(jnp.float32), axis=0)
    block_rank = rank // width_parts
    summed = lax.psum(partial_value, "tensor").astype(jnp.bfloat16)
    in_proj = summed[:, :rank]
    out_proj = summed[:, rank:]
    own_out = lax.dynamic_slice_in_dim(out_proj, position * block_rank, block_rank, 1)
    member = (seg_row[:, None] == labels[None, :]).astype(jnp.bfloat16)
    masked = (member[:, :, None] * own_out[:, None, :]).reshape(tok_rows, EX_DEV * block_rank)
    log_sums = jnp.einsum("ta,tj->aj", masked, in_proj, preferred_element_type=jnp.float32)
    log_sums = log_sums.reshape(EX_DEV, block_rank * rank)
    query_block = (log_sums / counts[:, None]).astype(jnp.bfloat16)
    train_full = lax.all_to_all(train_logs, "tensor", split_axis=0, concat_axis=1, tiled=True)
    local_rows = train_full.shape[0]
    wide_block = lax.all_gather(query_block, "tensor", axis=1, tiled=True)
    rows = lax.dot_general(
        lax.all_gather(wide_block, "dp", axis=0, tiled=True),
        train_full,
        (((1,), (1,)), ((), ())),
        preferred_element_type=jnp.float32,
    )
    scores = rows * 0.125
    doc_labels = jnp.arange(DOCS, dtype=jnp.int32)
    doc_hot = (doc_ids[:, None] == doc_labels[None, :]).astype(jnp.float32)
    doc_part = jnp.dot(scores, doc_hot, precision=lax.Precision.HIGHEST)
    total_rows = local_rows * lax.axis_size("tensor") * lax.axis_size("dp")
    doc_total = lax.psum(doc_part, ("dp", "tensor"))
    doc_influence = doc_total / math.sqrt(total_rows / DOCS)
    return (scores, doc_influence)


def solution(mesh):
    placed = (
        P("dp", "tensor"),
        P("dp", "tensor"),
        P("tensor", None),
        P("tensor", None),
        P("dp", None),
        P("dp", "tensor"),
        P(("dp", "tensor")),
    )
    return jax.shard_map(
        per_device,
        mesh=mesh,
        in_specs=placed,
        out_specs=(P(None, ("dp", "tensor")), P()),
        check_vma=False,
    )
```

profile of v0, /device:TPU:2, one launch (start us, length us, event | category | flops | bytes accessed | tf_op | source)
XLA Modules:
  0.0 761.5 jit_solution(6124716450737580398)
XLA Ops:
  7.2 0.0 copy-start
  7.2 0.0 all-gather.2.cloned.1.call-start
  7.2 0.9 convert_reduce_fusion
  8.1 0.7 fusion.4
  8.8 1.3 fusion.5
  10.1 1.7 fusion.6
  11.8 0.1 pad_maximum_fusion
  11.8 70.0 %all-reduce.4 = bf16[1024,128]{0,1:T(8,128)(2,1)S(1)} all-reduce(f32[1024,128]{0,1:T(8,128)S(1)} %pad_maximum_fusion), channel_id=1, replica_groups=mesh['dp'=32,'tensor'=16] {'tensor'}, use_global_device_ids=true, to_apply=%region_0.0 | all-reduce | flops 131072 | bytes 786432 | tf_op jit(solution)/shard_map/psum | solution.py:27
  81.9 0.1 broadcast_multiply_fusion.1
  82.0 0.1 mul.30
  82.0 0.2 fusion.1
  82.2 0.1 reshape.42
  82.3 0.1 divide_convert_fusion
  82.4 27.0 %all_gather.6 = bf16[24,4096]{1,0:T(8,128)(2,1)} all-gather(bf16[24,256]{1,0:T(8,128)(2,1)S(1)} %divide_convert_fusion), channel_id=1, replica_groups=mesh['dp'=32,'tensor'=16] {'tensor'}, dimensions={1}, use_global_device_ids=true | all-gather | bytes 208896 | tf_op jit(solution)/shard_map/all_gather | solution.py:38
  109.4 0.0 all-gather.2.cloned.1.call-update
  109.4 0.0 all-reduce.3.cloned.1.call-start
  109.4 34.0 %all_to_all.19 = bf16[16,256,256]{2,1,0:T(8,128)(2,1)S(1)} all-to-all(bf16[16,256,256]{2,1,0:T(8,128)(2,1)} %bitcast.15), channel_id=1, replica_groups=mesh['dp'=32,'tensor'=16] {'tensor'}, dimensions={0} | all-to-all | bytes 4194304 | tf_op jit(solution)/shard_map/all_to_all | solution.py:36
  143.5 2.4 copy.12
  145.9 133.8 %all-gather.2.cloned.1.call-done = bf16[768,4096]{1,0:T(8,128)(2,1)} async-done(((bf16[24,4096]{1,0:T(8,128)(2,1)}), bf16[768,4096]{1,0:T(8,128)(2,1)}) %all-gather.2.cloned.1.call-update) | async-done | bytes 6291472 | tf_op jit(solution)/shard_map/all_gather | solution.py:40
  279.7 5.2 convolution_multiply_fusion
  284.9 1.5 fusion
  286.4 0.0 all-reduce.3.cloned.1.call-update
  286.4 466.2 %all-reduce.3.cloned.1.call-done = f32[768,256]{1,0:T(8,128)} async-done(((f32[768,256]{1,0:T(8,128)}), f32[768,256]{1,0:T(8,128)}) %all-reduce.3.cloned.1.call-update) | async-done | bytes 786448 | tf_op jit(solution)/shard_map/psum | solution.py:50
  752.6 2.1 broadcast_multiply_fusion
  (7 shorter events, 0.0 us)
Async XLA Ops:
  7.2 1.7 copy-start
  7.2 272.5 %all-gather.2.cloned.1.call-start = ((), (), s32[]{:S(2)}) async-start(), calls=%async_computation.1 | async-start | bytes 6488064 | tf_op jit(solution)/shard_map/all_gather | solution.py:40
  109.4 643.2 %all-reduce.3.cloned.1.call-start = ((), (), s32[]{:S(2)}) async-start(), calls=%async_computation.2 | async-start | bytes 1572864 | tf_op jit(solution)/shard_map/psum | solution.py:50
  279.7 5.2 copy-start.2
  284.9 469.8 %copy-start.1 = (f32[768,256]{1,0:T(8,128)}, f32[768,256]{1,0:T(8,128)S(1)}, u32[]{:S(2)}) copy-start(f32[768,256]{1,0:T(8,128)S(1)} %convolution_multiply_fusion) | copy-start | bytes 2359300
Sparse Core Ops, SparseCore 0:
  109.5 170.1 all-gather.1
  286.5 466.0 all-reduce.2
where the time goes:
time: 762 us
  waiting for transfers between devices  600 us (79%)
  blocking collectives  131 us (17%)
  between operations  14.1 us (2%)
  matrix products  9.8 us (1%)
    psum x1, waiting for transfers between devices, per_device(): doc_total = lax.psum(doc_part, ('dp', 'tensor'))  466 us
    all_gather x1, waiting for transfers between devices, per_device(): lax.all_gather(wide_block, 'dp', axis=0, tiled=True)  134 us
    psum x1, blocking collectives, per_device(): summed = lax.psum(partial_value, 'tensor').astype(jnp.bfloat16)  70 us
    all_to_all x1, blocking collectives, per_device(): lax.all_to_all(train_logs, 'tensor', split_axis=0, concat_axis=1, tiled=T...  34 us
    all_gather x1, blocking collectives, per_device(): wide_block = lax.all_gather(query_block, 'tensor', axis=1, tiled=True)  27 us
  transfers between devices with their start and end apart: 2, of which 2 were waited for; matrix products, arithmetic and copies ran while one was open for 0% of the time, Pallas kernels for 0%

commit v1 on v0

--- a/solution.py
+++ b/solution.py
@@ -47,7 +47,8 @@
     doc_hot = (doc_ids[:, None] == doc_labels[None, :]).astype(jnp.float32)
     doc_part = jnp.dot(scores, doc_hot, precision=lax.Precision.HIGHEST)
     total_rows = local_rows * lax.axis_size("tensor") * lax.axis_size("dp")
-    doc_total = lax.psum(doc_part, ("dp", "tensor"))
+    inner = lax.psum(doc_part, "tensor")
+    doc_total = lax.psum(inner, "dp")
     doc_influence = doc_total / math.sqrt(total_rows / DOCS)
     return (scores, doc_influence)
 

time: 762 us -> 717 us (0.941)
  waiting for transfers between devices: 600 us -> 555 us
    psum x1 -> x2, waiting for transfers between devices: 466 us -> 422 us  [the longest x1 273 us: per_device(): doc_total = lax.psum(inner, 'dp')]
  transfers between devices with their start and end apart: 2 -> 3, of which waited for: 2 -> 3; matrix products, arithmetic and copies ran while one was open for 0% -> 0% of each run, Pallas kernels for 0% -> 0%
where the time goes in v1:
time: 717 us; the launch traced here: 716 us
  waiting for transfers between devices  555 us (77%)
  blocking collectives  131 us (18%)
  between operations  13.9 us (2%)
  matrix products  9.8 us (1%)
    psum x1, waiting for transfers between devices, per_device(): doc_total = lax.psum(inner, 'dp')  273 us
    psum x1, waiting for transfers between devices, per_device(): inner = lax.psum(doc_part, 'tensor')  149 us
    all_gather x1, waiting for transfers between devices, per_device(): lax.all_gather(wide_block, 'dp', axis=0, tiled=True)  133 us
    psum x1, blocking collectives, per_device(): summed = lax.psum(partial_value, 'tensor').astype(jnp.bfloat16)  70 us
    all_to_all x1, blocking collectives, per_device(): lax.all_to_all(train_logs, 'tensor', split_axis=0, concat_axis=1, tiled=T...  34 us
    all_gather x1, blocking collectives, per_device(): wide_block = lax.all_gather(query_block, 'tensor', axis=1, tiled=True)  27 us
  transfers between devices with their start and end apart: 3, of which 3 were waited for; matrix products, arithmetic and copies ran while one was open for 0% of the time, Pallas kernels for 0%

profile of v1, /device:TPU:2, one launch (start us, length us, event | category | flops | bytes accessed | tf_op | source)
XLA Modules:
  0.0 716.2 jit_solution(8600586204356548174)
XLA Ops:
  7.2 0.0 all-gather.2.cloned.1.call-start
  7.2 0.9 convert_reduce_fusion
  8.1 0.7 fusion.4
  8.8 1.3 fusion.5
  10.1 1.7 fusion.6
  11.8 0.1 pad_maximum_fusion
  11.8 70.0 %all-reduce.7 = bf16[1024,128]{0,1:T(8,128)(2,1)S(1)} all-reduce(f32[1024,128]{0,1:T(8,128)S(1)} %pad_maximum_fusion), channel_id=1, replica_groups=mesh['dp'=32,'tensor'=16] {'tensor'}, use_global_device_ids=true, to_apply=%region_0.0 | all-reduce | flops 131072 | bytes 786432 | tf_op jit(solution)/shard_map/psum | solution.py:27
  81.9 0.1 broadcast_multiply_fusion.1
  82.0 0.1 mul.30
  82.0 0.2 fusion.1
  82.2 0.1 reshape.42
  82.3 0.1 divide_convert_fusion
  82.4 27.0 %all_gather.6 = bf16[24,4096]{1,0:T(8,128)(2,1)} all-gather(bf16[24,256]{1,0:T(8,128)(2,1)S(1)} %divide_convert_fusion), channel_id=1, replica_groups=mesh['dp'=32,'tensor'=16] {'tensor'}, dimensions={1}, use_global_device_ids=true | all-gather | bytes 208896 | tf_op jit(solution)/shard_map/all_gather | solution.py:38
  109.4 0.0 all-gather.2.cloned.1.call-update
  109.4 0.0 all-reduce.4.cloned.1.call-start
  109.4 34.0 %all_to_all.19 = bf16[16,256,256]{2,1,0:T(8,128)(2,1)S(1)} all-to-all(bf16[16,256,256]{2,1,0:T(8,128)(2,1)} %bitcast.15), channel_id=1, replica_groups=mesh['dp'=32,'tensor'=16] {'tensor'}, dimensions={0} | all-to-all | bytes 4194304 | tf_op jit(solution)/shard_map/all_to_all | solution.py:36
  143.5 2.4 copy.12
  145.9 133.4 %all-gather.2.cloned.1.call-done = bf16[768,4096]{1,0:T(8,128)(2,1)} async-done(((bf16[24,4096]{1,0:T(8,128)(2,1)}), bf16[768,4096]{1,0:T(8,128)(2,1)}) %all-gather.2.cloned.1.call-update) | async-done | bytes 6291472 | tf_op jit(solution)/shard_map/all_gather | solution.py:40
  279.2 5.2 convolution_multiply_fusion
  284.5 1.5 fusion
  286.0 0.0 all-reduce.6.cloned.1.call-start
  286.0 148.7 %all-reduce.4.cloned.1.call-done = f32[768,256]{1,0:T(8,128)} async-done(((f32[768,256]{1,0:T(8,128)}), f32[768,256]{1,0:T(8,128)}) %all-reduce.4.cloned.1.call-update) | async-done | bytes 786448 | tf_op jit(solution)/shard_map/psum | solution.py:50
  434.8 272.8 %all-reduce.6.cloned.1.call-done = f32[768,256]{1,0:T(8,128)} async-done(((f32[768,256]{1,0:T(8,128)}), f32[768,256]{1,0:T(8,128)}) %all-reduce.6.cloned.1.call-update) | async-done | bytes 786448 | tf_op jit(solution)/shard_map/psum | solution.py:51
  707.6 2.1 broadcast_multiply_fusion
  (10 shorter events, 0.1 us)
Async XLA Ops:
  7.2 1.7 copy-start
  7.2 272.1 %all-gather.2.cloned.1.call-start = ((), (), s32[]{:S(2)}) async-start(), calls=%async_computation.1 | async-start | bytes 6488064 | tf_op jit(solution)/shard_map/all_gather | solution.py:40
  109.4 325.4 %all-reduce.4.cloned.1.call-start = ((), (), s32[]{:S(2)}) async-start(), calls=%async_computation.2 | async-start | bytes 1572864 | tf_op jit(solution)/shard_map/psum | solution.py:50
  279.2 5.2 copy-start.2
  284.5 425.2 %copy-start.1 = (f32[768,256]{1,0:T(8,128)}, f32[768,256]{1,0:T(8,128)S(1)}, u32[]{:S(2)}) copy-start(f32[768,256]{1,0:T(8,128)S(1)} %convolution_multiply_fusion) | copy-start | bytes 2359300
  286.0 421.6 %all-reduce.6.cloned.1.call-start = ((), (), s32[]{:S(2)}) async-start(), calls=%async_computation.3 | async-start | bytes 1572864 | tf_op jit(solution)/shard_map/psum | solution.py:51
Sparse Core Ops, SparseCore 0:
  109.5 169.6 all-gather.1
  286.1 148.6 all-reduce.3
  437.9 269.6 all-reduce.5
